TPU v7x, 32 devices: a whole 2x2x4 slice. The times are simulated.
32 devices in a mesh: view: 4 (over y, core), row: 8 (over z, x).
Axes of the slice: x: 2, y: 2, z: 4, core: 2. Of those that a mesh axis runs over, the one named last changes fastest.
Arguments:
- features: float32 [4, 16384, 2048], P('view', 'row'), may hold values from -0.125 to 0.125
- view_maps: float32 [4, 2048, 256], P('view', 'row'), may hold values from -6 to 6
- shared: float32 [16384, 256], P('row'), may hold values from -6 to 6
Outputs:
- maps_out: float32 [4, 2048, 256], P('view', 'row')
- shared_out: float32 [16384, 256], P('row')
All inputs are finite; a program needn't handle non-finite values.
Results may differ from a plain program's by a relative error of at most 0.00013.
Values sent between devices are 32-bit elements; how exact they have to be, the bound alone decides.
A program may use at most 128 MiB of HBM per device.

v0:
```python
import jax
import jax.numpy as jnp
from jax import lax
from jax.sharding import PartitionSpec as P

ITERS = 2
NEWTON = 5
step_rate = 0.5


def newton_root(gram_matrix):
    highest = lax.Precision.HIGHEST
    frob_norm = jnp.sqrt(jnp.sum(gram_matrix * gram_matrix))
    scaled = gram_matrix / frob_norm
    identity = jnp.eye(gram_matrix.shape[0], dtype=jnp.float32)
    inverse_root = identity
    for newton_step in range(NEWTON):
        correction = 1.5 * identity - 0.5 * jnp.dot(inverse_root, scaled, precision=highest)
        scaled = jnp.dot(scaled, correction, precision=highest)
        inverse_root = jnp.dot(correction, inverse_root, precision=highest)
    return (inverse_root, frob_norm)


def local(features, view_maps, shared):
    highest = lax.Precision.HIGHEST
    samples = features[0]
    map_shard = view_maps[0]
    local_rows = samples.shape[0]
    width = samples.shape[1]
    shard_rows = map_shard.shape[0]
    total_rows = local_rows * lax.axis_size("row")
    view_count = lax.axis_size("view")
    step_size = step_rate * width / total_rows
    whole_map = lax.all_gather(map_shard, "row", axis=0, tiled=True)
    projected = jnp.dot(samples, whole_map, precision=highest)
    for iteration in range(ITERS):
        residual = projected - shared
        gradient = lax.psum(jnp.dot(samples.T, residual, precision=highest), "row")
        whole_map = whole_map - step_size * gradient
        projected = jnp.dot(samples, whole_map, precision=highest)
        average = lax.psum(projected, "view") / view_count
        gram_matrix = lax.psum(jnp.dot(average.T, average, precision=highest), "row")
        inverse_root, frob_norm = newton_root(gram_matrix)
        shared = jnp.dot(average, inverse_root, precision=highest) * jnp.sqrt(
            total_rows / frob_norm
        )
    map_shard = lax.dynamic_slice_in_dim(
        whole_map, lax.axis_index("row") * shard_rows, shard_rows, 0
    )
    return (map_shard[None], shared)


def solution(mesh):
    in_specs = (P("view", "row", None), P("view", "row", None), P("row", None))
    out_specs = (P("view", "row", None), P("row", None))
    return jax.shard_map(local, mesh=mesh, in_specs=in_specs, out_specs=out_specs, check_vma=False)
```

profile of v0, /device:TPU:0, one launch (start us, length us, event | category | flops | bytes accessed | tf_op | source)
XLA Modules:
  0.0 663.0 jit_solution(7803501747945105830)
XLA Ops:
  7.2 1.8 copy.6
  9.1 54.6 %all-gather.3.cloned.1.call-done = f32[1,2048,256]{1,2,0:T(8,128)} async-done(((f32[1,256,256]{1,2,0:T(8,128)}), f32[1,2048,256]{1,2,0:T(8,128)}) %all-gather.3.cloned.1.call-update) | async-done | bytes 2097168 | tf_op jit(solution)/shard_map/all_gather | solution.py:34
  63.7 17.4 %fusion.23 = f32[2048,256]{1,0:T(8,128)S(1)} fusion(f32[2048,256]{1,0:T(8,128)} %param.5, f32[1,2048,2048]{2,1,0:T(8,128)} %param.3, f32[1,2048,256]{1,2,0:T(8,128)} %all-gather.3.cloned.1.call-done), kind=kOutput, calls=%fused_computation.17 | convolution fusion | flops 12885426176 | bytes 23068672 | tf_op jit(solution)/shard_map/dot_general | solution.py:35
  81.1 31.3 %fusion.10 = f32[2048,256]{0,1:T(8,128)} fusion(f32[2048,256]{1,0:T(8,128)S(1)} %fusion.23, f32[1,2048,2048]{2,1,0:T(8,128)S(1)} %copy-done), kind=kOutput, calls=%fused_computation.10 | convolution fusion | flops 12884901888 | bytes 20971520 | tf_op jit(solution)/shard_map/dot_general | solution.py:38
  112.5 100.6 %all-reduce.7.cloned.1.call-done = f32[2048,256]{0,1:T(8,128)} async-done(((f32[2048,256]{0,1:T(8,128)}), f32[2048,256]{0,1:T(8,128)}) %all-reduce.7.cloned.1.call-update) | async-done | bytes 2097168 | tf_op jit(solution)/shard_map/psum | solution.py:38
  213.1 18.8 %fusion.13 = f32[2048,256]{0,1:T(8,128)} fusion(f32[1,2048,2048]{2,1,0:T(8,128)} %param.3, f32[1,2048,256]{1,2,0:T(8,128)S(1)} %copy-done.1, f32[2048,256]{0,1:T(8,128)} %all-reduce.7.cloned.1.call-done), kind=kOutput, calls=%fused_computation.11 | convolution fusion | flops 12885950464 | bytes 23068672 | tf_op jit(solution)/shard_map/dot_general | solution.py:40
  232.0 50.8 %all-reduce.9.cloned.1.call-done = f32[2048,256]{0,1:T(8,128)} async-done(((f32[2048,256]{0,1:T(8,128)}), f32[2048,256]{0,1:T(8,128)}) %all-reduce.9.cloned.1.call-update) | async-done | bytes 2097168 | tf_op jit(solution)/shard_map/psum | solution.py:41
  282.8 4.9 fusion.31
  287.7 71.2 %all-reduce.11.cloned.1.call-done = f32[256,256]{1,0:T(8,128)} async-done(((f32[256,256]{1,0:T(8,128)}), f32[256,256]{1,0:T(8,128)}) %all-reduce.11.cloned.1.call-update) | async-done | bytes 262160 | tf_op jit(solution)/shard_map/psum | solution.py:42
  358.9 1.6 multiply_reduce_fusion.1
  361.3 1.3 fusion.42
  362.8 1.3 fusion.49
  365.3 0.4 fusion.40
  366.5 0.4 fusion.39
  367.6 0.4 fusion.38
  368.5 4.4 fusion.22
  372.9 17.8 %fusion.16 = f32[2048,256]{0,1:T(8,128)} fusion(f32[2048,256]{0,1:T(8,128)S(1)} %fusion.22, f32[1,2048,2048]{2,1,0:T(8,128)} %param.3), kind=kOutput, calls=%fused_computation.12 | convolution fusion | flops 12884901888 | bytes 20971520 | tf_op jit(solution)/shard_map/dot_general | solution.py:38
  390.7 101.6 %all-reduce.13.cloned.1.call-done = f32[2048,256]{0,1:T(8,128)} async-done(((f32[2048,256]{0,1:T(8,128)}), f32[2048,256]{0,1:T(8,128)}) %all-reduce.13.cloned.1.call-update) | async-done | bytes 2097168 | tf_op jit(solution)/shard_map/psum | solution.py:38
  492.4 2.8 multiply_subtract_fusion
  495.2 1.3 copy-done.2
  496.5 17.9 %fusion.19 = f32[2048,256]{0,1:T(8,128)} fusion(f32[2048,256]{0,1:T(8,128)S(1)} %multiply_subtract_fusion, f32[1,2048,2048]{2,1,0:T(8,128)} %param.3), kind=kOutput, calls=%fused_computation.13 | convolution fusion | flops 12884901888 | bytes 20971520 | tf_op jit(solution)/shard_map/dot_general | solution.py:40
  514.7 50.6 %all-reduce.15.cloned.1.call-done = f32[2048,256]{0,1:T(8,128)} async-done(((f32[2048,256]{0,1:T(8,128)}), f32[2048,256]{0,1:T(8,128)}) %all-reduce.15.cloned.1.call-update) | async-done | bytes 2097168 | tf_op jit(solution)/shard_map/psum | solution.py:41
  565.2 4.9 fusion.28
  570.1 1.0 constant_dynamic-slice_fusion
  571.1 0.8 copy.7
  572.0 69.4 %all-reduce.17.cloned.1.call-done = f32[256,256]{1,0:T(8,128)} async-done(((f32[256,256]{1,0:T(8,128)}), f32[256,256]{1,0:T(8,128)}) %all-reduce.17.cloned.1.call-update) | async-done | bytes 262160 | tf_op jit(solution)/shard_map/psum | solution.py:42
  641.4 1.6 multiply_reduce_fusion
  643.7 1.3 fusion.37
  645.3 1.3 fusion.50
  647.8 0.4 fusion.35
  650.2 0.4 fusion.33
  651.0 4.8 convolution_multiply_fusion
  (40 shorter events, 7.6 us)
Async XLA Ops:
  7.2 56.5 %all-gather.3.cloned.1.call-start = ((), (), s32[]{:S(2)}) async-start(), calls=%async_computation.6 | async-start | bytes 2359296 | tf_op jit(solution)/shard_map/all_gather | solution.py:34
  9.0 204.1 %all-reduce.7.cloned.1.call-start = ((), (), s32[]{:S(2)}) async-start(), calls=%async_computation | async-start | bytes 4194304 | tf_op jit(solution)/shard_map/psum | solution.py:38
  63.7 17.4 %copy-start = (f32[1,2048,2048]{2,1,0:T(8,128)S(1)}, f32[1,2048,2048]{2,1,0:T(8,128)}, u32[]{:S(2)}) copy-start(f32[1,2048,2048]{2,1,0:T(8,128)} %param.3) | copy-start | bytes 50331652
  112.4 100.7 %copy-start.1 = (f32[1,2048,256]{1,2,0:T(8,128)S(1)}, f32[1,2048,256]{1,2,0:T(8,128)}, u32[]{:S(2)}) copy-start(f32[1,2048,256]{1,2,0:T(8,128)} %all-gather.3.cloned.1.call-done) | copy-start | bytes 6291460
  112.4 170.4 %all-reduce.9.cloned.1.call-start = ((), (), s32[]{:S(2)}) async-start(), calls=%async_computation.1 | async-start | bytes 4194304 | tf_op jit(solution)/shard_map/psum | solution.py:41
  231.9 127.0 %all-reduce.11.cloned.1.call-start = ((), (), s32[]{:S(2)}) async-start(), calls=%async_computation.2 | async-start | bytes 524288 | tf_op jit(solution)/shard_map/psum | solution.py:42
  287.7 204.7 %all-reduce.13.cloned.1.call-start = ((), (), s32[]{:S(2)}) async-start(), calls=%async_computation.3 | async-start | bytes 4194304 | tf_op jit(solution)/shard_map/psum | solution.py:38
  390.7 174.6 %all-reduce.15.cloned.1.call-start = ((), (), s32[]{:S(2)}) async-start(), calls=%async_computation.4 | async-start | bytes 4194304 | tf_op jit(solution)/shard_map/psum | solution.py:41
  495.2 1.3 copy-start.2
  514.4 127.0 %all-reduce.17.cloned.1.call-start = ((), (), s32[]{:S(2)}) async-start(), calls=%async_computation.5 | async-start | bytes 524288 | tf_op jit(solution)/shard_map/psum | solution.py:42
  648.9 2.0 copy-start.3
Sparse Core Ops, SparseCore 0:
  10.6 53.0 all-gather.2
  112.5 100.5 all-reduce.6
  232.1 50.6 all-reduce.8
  287.8 71.0 all-reduce.10
  390.8 101.5 all-reduce.12
  514.5 50.6 all-reduce.14
  570.3 71.0 all-reduce.16
where the time goes:
time: 667 us; the launch traced here: 663 us
  waiting for transfers between devices  499 us (75%)
  matrix products  136 us (20%)
  between operations  16.4 us (2%)
    psum x2, waiting for transfers between devices, local(): gradient = lax.psum(jnp.dot(samples.T, residual, precision=highest), 'row')  202 us
    psum x2, waiting for transfers between devices, local(): lax.psum(jnp.dot(average.T, average, precision=highest), 'row')  141 us
    psum x2, waiting for transfers between devices, local(): average = lax.psum(projected, 'view') / view_count  101 us
    all_gather x1, waiting for transfers between devices, local(): whole_map = lax.all_gather(map_shard, 'row', axis=0, tiled=True)  54.6 us
    dot_general x3, matrix products, local(): projected = jnp.dot(samples, whole_map, precision=highest)  54.1 us
    dot_general x2, matrix products, local(): gradient = lax.psum(jnp.dot(samples.T, residual, precision=highest), 'row')  49.1 us
  transfers between devices with their start and end apart: 7, of which 7 were waited for; matrix products, arithmetic and copies ran while one was open for 0% of the time, Pallas kernels for 0%

commit v1 on v0

--- a/solution.py
+++ b/solution.py
@@ -1,11 +1,27 @@
+import functools
 import jax
 import jax.numpy as jnp
 from jax import lax
 from jax.sharding import PartitionSpec as P
+from jax.lax import axis_index, ppermute, psum
 
 ITERS = 2
 NEWTON = 5
 step_rate = 0.5
+
+
+def limits_register(vals, axis_k):
+    n_blocks = psum(1, "row")
+    all_rows = [vals]
+    for dd in range(n_blocks - 1):
+        all_rows.append(
+            ppermute(all_rows[-1], "row", [(w, (w + 1) % n_blocks) for w in range(n_blocks)])
+        )
+    tile_out = jnp.concatenate(all_rows[::-1], axis=axis_k)
+    return jnp.roll(tile_out, shift=(axis_index("row") + 1) * vals.shape[axis_k], axis=axis_k)
+
+
+bind_classes = functools.partial(limits_register, axis_k=0)
 
 
 def newton_root(gram_matrix):
@@ -31,7 +47,7 @@
     total_rows = local_rows * lax.axis_size("row")
     view_count = lax.axis_size("view")
     step_size = step_rate * width / total_rows
-    whole_map = lax.all_gather(map_shard, "row", axis=0, tiled=True)
+    whole_map = bind_classes(map_shard)
     projected = jnp.dot(samples, whole_map, precision=highest)
     for iteration in range(ITERS):
         residual = projected - shared

time: 667 us -> 684 us (1.025)
  waiting for transfers between devices: 499 us -> 509 us
    ppermute x0 -> x7, waiting for transfers between devices: none -> 65.7 us  [limits_register(): ppermute(all_rows[-1], 'row', [(w, (w + 1) % n_blocks) for w in range(n_b...]
    all_gather x1 -> x0, waiting for transfers between devices: 54.6 us -> none  [local(): whole_map = lax.all_gather(map_shard, 'row', axis=0, tiled=True)]
  transfers between devices with their start and end apart: 7 -> 13, of which waited for: 7 -> 13; matrix products, arithmetic and copies ran while one was open for 0% -> 0% of each run, Pallas kernels for 0% -> 0%
where the time goes in v1:
time: 684 us; the launch traced here: 678 us
  waiting for transfers between devices  509 us (74%)
  matrix products  137 us (20%)
  between operations  16.5 us (2%)
    psum x2, waiting for transfers between devices, local(): gradient = lax.psum(jnp.dot(samples.T, residual, precision=highest), 'row')  201 us
    psum x2, waiting for transfers between devices, local(): lax.psum(jnp.dot(average.T, average, precision=highest), 'row')  141 us
    psum x2, waiting for transfers between devices, local(): average = lax.psum(projected, 'view') / view_count  101 us
    ppermute x7, waiting for transfers between devices, limits_register(): ppermute(all_rows[-1], 'row', [(w, (w + 1) % n_blocks) for w in range(n_b...  65.7 us
    dot_general x3, matrix products, local(): projected = jnp.dot(samples, whole_map, precision=highest)  55.9 us
    dot_general x2, matrix products, local(): gradient = lax.psum(jnp.dot(samples.T, residual, precision=highest), 'row')  49.1 us
  transfers between devices with their start and end apart: 13, of which 13 were waited for; matrix products, arithmetic and copies ran while one was open for 0% of the time, Pallas kernels for 0%

profile of v1, /device:TPU:0, one launch (start us, length us, event | category | flops | bytes accessed | tf_op | source)
XLA Modules:
  0.0 678.4 jit_solution(6600533347301761493)
XLA Ops:
  8.3 3.0 collective-permute-start
  11.3 9.3 %collective-permute-done = f32[256,256]{0,1:T(8,128)S(1)} collective-permute-done((f32[256,256]{0,1:T(8,128)S(1)}, f32[256,256]{0,1:T(8,128)S(1)}, u32[]{:S(2)}, u32[]{:S(2)}) %collective-permute-start) | collective-permute-done | bytes 262176 | tf_op jit(solution)/shard_map/ppermute | solution.py:18
  20.7 10.2 %collective-permute-done.1 = f32[256,256]{0,1:T(8,128)S(1)} collective-permute-done((f32[256,256]{0,1:T(8,128)S(1)}, f32[256,256]{0,1:T(8,128)S(1)}, u32[]{:S(2)}, u32[]{:S(2)}) %collective-permute-start.1) | collective-permute-done | bytes 262176 | tf_op jit(solution)/shard_map/ppermute | solution.py:18
  30.8 9.3 %collective-permute-done.2 = f32[256,256]{0,1:T(8,128)S(1)} collective-permute-done((f32[256,256]{0,1:T(8,128)S(1)}, f32[256,256]{0,1:T(8,128)S(1)}, u32[]{:S(2)}, u32[]{:S(2)}) %collective-permute-start.2) | collective-permute-done | bytes 262176 | tf_op jit(solution)/shard_map/ppermute | solution.py:18
  40.1 9.1 %collective-permute-done.3 = f32[256,256]{0,1:T(8,128)S(1)} collective-permute-done((f32[256,256]{0,1:T(8,128)S(1)}, f32[256,256]{0,1:T(8,128)S(1)}, u32[]{:S(2)}, u32[]{:S(2)}) %collective-permute-start.3) | collective-permute-done | bytes 262176 | tf_op jit(solution)/shard_map/ppermute | solution.py:18
  49.2 9.1 %collective-permute-done.4 = f32[256,256]{0,1:T(8,128)S(1)} collective-permute-done((f32[256,256]{0,1:T(8,128)S(1)}, f32[256,256]{0,1:T(8,128)S(1)}, u32[]{:S(2)}, u32[]{:S(2)}) %collective-permute-start.4) | collective-permute-done | bytes 262176 | tf_op jit(solution)/shard_map/ppermute | solution.py:18
  58.3 9.7 %collective-permute-done.5 = f32[256,256]{0,1:T(8,128)S(1)} collective-permute-done((f32[256,256]{0,1:T(8,128)S(1)}, f32[256,256]{0,1:T(8,128)S(1)}, u32[]{:S(2)}, u32[]{:S(2)}) %collective-permute-start.5) | collective-permute-done | bytes 262176 | tf_op jit(solution)/shard_map/ppermute | solution.py:18
  68.0 9.1 %collective-permute-done.6 = f32[256,256]{0,1:T(8,128)S(1)} collective-permute-done((f32[256,256]{0,1:T(8,128)S(1)}, f32[256,256]{0,1:T(8,128)S(1)}, u32[]{:S(2)}, u32[]{:S(2)}) %collective-permute-start.6) | collective-permute-done | bytes 262176 | tf_op jit(solution)/shard_map/ppermute | solution.py:18
  77.6 1.3 copy-done.5
  78.9 18.7 %fusion.26 = f32[2048,256]{1,0:T(8,128)S(1)} fusion(f32[2048,256]{1,0:T(8,128)S(1)} %copy-done.5, f32[1,2048,2048]{2,1,0:T(8,128)} %param.3, f32[4096,256]{0,1:T(8,128)S(1)} %constant_dynamic-update-slice_fusion, s32[]{:T(128)S(6)} %select_n.17), kind=kOutput, calls=%fused_computation.18 | convolution fusion | flops 12885426176 | bytes 23068676 | tf_op jit(solution)/shard_map/dot_general | solution.py:51
  97.6 31.3 %fusion.13 = f32[2048,256]{0,1:T(8,128)} fusion(f32[2048,256]{1,0:T(8,128)S(1)} %fusion.26, f32[1,2048,2048]{2,1,0:T(8,128)S(1)} %bitcast.93), kind=kOutput, calls=%fused_computation.11 | convolution fusion | flops 12884901888 | bytes 20971520 | tf_op jit(solution)/shard_map/dot_general | solution.py:54
  129.1 99.5 %all-reduce.7.cloned.1.call-done = f32[2048,256]{0,1:T(8,128)} async-done(((f32[2048,256]{0,1:T(8,128)}), f32[2048,256]{0,1:T(8,128)}) %all-reduce.7.cloned.1.call-update) | async-done | bytes 2097168 | tf_op jit(solution)/shard_map/psum | solution.py:54
  228.6 19.4 %fusion.16 = f32[2048,256]{0,1:T(8,128)} fusion(f32[1,2048,2048]{2,1,0:T(8,128)} %param.3, f32[2048,256]{0,1:T(8,128)} %all-reduce.7.cloned.1.call-done, f32[4096,256]{0,1:T(8,128)} %copy-done.3, s32[]{:T(128)S(6)} %select_n.17), kind=kOutput, calls=%fused_computation.12 | convolution fusion | flops 12885950464 | bytes 23068676 | tf_op jit(solution)/shard_map/dot_general | solution.py:56
  248.1 50.8 %all-reduce.9.cloned.1.call-done = f32[2048,256]{0,1:T(8,128)} async-done(((f32[2048,256]{0,1:T(8,128)}), f32[2048,256]{0,1:T(8,128)}) %all-reduce.9.cloned.1.call-update) | async-done | bytes 2097168 | tf_op jit(solution)/shard_map/psum | solution.py:57
  298.8 4.9 fusion.33
  303.8 71.2 %all-reduce.11.cloned.1.call-done = f32[256,256]{1,0:T(8,128)} async-done(((f32[256,256]{1,0:T(8,128)}), f32[256,256]{1,0:T(8,128)}) %all-reduce.11.cloned.1.call-update) | async-done | bytes 262160 | tf_op jit(solution)/shard_map/psum | solution.py:58
  375.0 1.6 multiply_reduce_fusion.1
  377.3 1.3 fusion.45
  378.9 1.3 fusion.52
  384.6 3.7 fusion.25
  388.3 17.8 %fusion.19 = f32[2048,256]{0,1:T(8,128)} fusion(f32[2048,256]{0,1:T(8,128)S(1)} %fusion.25, f32[1,2048,2048]{2,1,0:T(8,128)} %param.3), kind=kOutput, calls=%fused_computation.13 | convolution fusion | flops 12884901888 | bytes 20971520 | tf_op jit(solution)/shard_map/dot_general | solution.py:54
  406.2 101.6 %all-reduce.13.cloned.1.call-done = f32[2048,256]{0,1:T(8,128)} async-done(((f32[2048,256]{0,1:T(8,128)}), f32[2048,256]{0,1:T(8,128)}) %all-reduce.13.cloned.1.call-update) | async-done | bytes 2097168 | tf_op jit(solution)/shard_map/psum | solution.py:54
  507.8 2.8 multiply_subtract_fusion
  510.7 1.3 copy-done.2
  512.0 17.8 %fusion.22 = f32[2048,256]{0,1:T(8,128)} fusion(f32[2048,256]{0,1:T(8,128)S(1)} %multiply_subtract_fusion, f32[1,2048,2048]{2,1,0:T(8,128)} %param.3), kind=kOutput, calls=%fused_computation.14 | convolution fusion | flops 12884901888 | bytes 20971520 | tf_op jit(solution)/shard_map/dot_general | solution.py:56
  530.1 50.6 %all-reduce.15.cloned.1.call-done = f32[2048,256]{0,1:T(8,128)} async-done(((f32[2048,256]{0,1:T(8,128)}), f32[2048,256]{0,1:T(8,128)}) %all-reduce.15.cloned.1.call-update) | async-done | bytes 2097168 | tf_op jit(solution)/shard_map/psum | solution.py:57
  580.6 4.9 fusion.30
  587.4 69.4 %all-reduce.17.cloned.1.call-done = f32[256,256]{1,0:T(8,128)} async-done(((f32[256,256]{1,0:T(8,128)}), f32[256,256]{1,0:T(8,128)}) %all-reduce.17.cloned.1.call-update) | async-done | bytes 262160 | tf_op jit(solution)/shard_map/psum | solution.py:58
  656.8 1.6 multiply_reduce_fusion
  659.2 1.3 fusion.40
  660.7 1.3 fusion.53
  666.4 4.8 convolution_multiply_fusion
  (80 shorter events, 12.8 us)
Async XLA Ops:
  7.2 221.4 %all-reduce.7.cloned.1.call-start = ((), (), s32[]{:S(2)}) async-start(), calls=%async_computation | async-start | bytes 4194304 | tf_op jit(solution)/shard_map/psum | solution.py:54
  8.3 12.4 %collective-permute-start = (f32[256,256]{0,1:T(8,128)S(1)}, f32[256,256]{0,1:T(8,128)S(1)}, u32[]{:S(2)}, u32[]{:S(2)}) collective-permute-start(f32[256,256]{0,1:T(8,128)S(1)} %bitcast.94), channel_id=1, source_target_pairs={{0,1},{1,2},{2,3},{3,4},{4,5},{5,6},{6,7},{7,0},{8,9},{9,10},{10,1... | collective-permute-start | bytes 786440 | tf_op jit(solution)/shard_map/ppermute | solution.py:18
  20.7 10.2 %collective-permute-start.1 = (f32[256,256]{0,1:T(8,128)S(1)}, f32[256,256]{0,1:T(8,128)S(1)}, u32[]{:S(2)}, u32[]{:S(2)}) collective-permute-start(f32[256,256]{0,1:T(8,128)S(1)} %collective-permute-done), channel_id=1, source_target_pairs={{0,1},{1,2},{2,3},{3,4},{4,5},{5,6},{6,7},{7,0},{8,9},{9,10},{10,1... | collective-permute-start | bytes 786440 | tf_op jit(solution)/shard_map/ppermute | solution.py:18
  30.8 9.3 %collective-permute-start.2 = (f32[256,256]{0,1:T(8,128)S(1)}, f32[256,256]{0,1:T(8,128)S(1)}, u32[]{:S(2)}, u32[]{:S(2)}) collective-permute-start(f32[256,256]{0,1:T(8,128)S(1)} %collective-permute-done.1), channel_id=1, source_target_pairs={{0,1},{1,2},{2,3},{3,4},{4,5},{5,6},{6,7},{7,0},{8,9},{9,10},{10,1... | collective-permute-start | bytes 786440 | tf_op jit(solution)/shard_map/ppermute | solution.py:18
  40.1 9.1 %collective-permute-start.3 = (f32[256,256]{0,1:T(8,128)S(1)}, f32[256,256]{0,1:T(8,128)S(1)}, u32[]{:S(2)}, u32[]{:S(2)}) collective-permute-start(f32[256,256]{0,1:T(8,128)S(1)} %collective-permute-done.2), channel_id=1, source_target_pairs={{0,1},{1,2},{2,3},{3,4},{4,5},{5,6},{6,7},{7,0},{8,9},{9,10},{10,1... | collective-permute-start | bytes 786440 | tf_op jit(solution)/shard_map/ppermute | solution.py:18
  49.2 9.1 %collective-permute-start.4 = (f32[256,256]{0,1:T(8,128)S(1)}, f32[256,256]{0,1:T(8,128)S(1)}, u32[]{:S(2)}, u32[]{:S(2)}) collective-permute-start(f32[256,256]{0,1:T(8,128)S(1)} %collective-permute-done.3), channel_id=1, source_target_pairs={{0,1},{1,2},{2,3},{3,4},{4,5},{5,6},{6,7},{7,0},{8,9},{9,10},{10,1... | collective-permute-start | bytes 786440 | tf_op jit(solution)/shard_map/ppermute | solution.py:18
  58.3 9.7 %collective-permute-start.5 = (f32[256,256]{0,1:T(8,128)S(1)}, f32[256,256]{0,1:T(8,128)S(1)}, u32[]{:S(2)}, u32[]{:S(2)}) collective-permute-start(f32[256,256]{0,1:T(8,128)S(1)} %collective-permute-done.4), channel_id=1, source_target_pairs={{0,1},{1,2},{2,3},{3,4},{4,5},{5,6},{6,7},{7,0},{8,9},{9,10},{10,1... | collective-permute-start | bytes 786440 | tf_op jit(solution)/shard_map/ppermute | solution.py:18
  68.0 9.1 %collective-permute-start.6 = (f32[256,256]{0,1:T(8,128)S(1)}, f32[256,256]{0,1:T(8,128)S(1)}, u32[]{:S(2)}, u32[]{:S(2)}) collective-permute-start(f32[256,256]{0,1:T(8,128)S(1)} %collective-permute-done.5), channel_id=1, source_target_pairs={{0,1},{1,2},{2,3},{3,4},{4,5},{5,6},{6,7},{7,0},{8,9},{9,10},{10,1... | collective-permute-start | bytes 786440 | tf_op jit(solution)/shard_map/ppermute | solution.py:18
  77.3 1.6 copy-start.5
  77.6 20.0 %slice-start = ((s8[16777216]{0:T(1024)(128)(4,1)}), s8[4194304]{0:T(1024)(128)(4,1)S(1)}, s32[]{:S(2)}) async-start(s8[16777216]{0:T(1024)(128)(4,1)} %bitcast.92), calls=%async_computation.6 | async-start | bytes 8388608
  78.9 18.7 %copy-start.3 = (f32[4096,256]{0,1:T(8,128)}, f32[4096,256]{0,1:T(8,128)S(1)}, u32[]{:S(2)}) copy-start(f32[4096,256]{0,1:T(8,128)S(1)} %constant_dynamic-update-slice_fusion) | copy-start | bytes 12582916
  78.9 18.7 %slice-start.1 = ((s8[16777216]{0:T(1024)(128)(4,1)}), s8[4194304]{0:T(1024)(128)(4,1)S(1)}, s32[]{:S(2)}) async-start(s8[16777216]{0:T(1024)(128)(4,1)} %bitcast.92), calls=%async_computation.7 | async-start | bytes 8388608
  78.9 18.7 %slice-start.2 = ((s8[16777216]{0:T(1024)(128)(4,1)}), s8[4194304]{0:T(1024)(128)(4,1)S(1)}, s32[]{:S(2)}) async-start(s8[16777216]{0:T(1024)(128)(4,1)} %bitcast.92), calls=%async_computation.8 | async-start | bytes 8388608
  78.9 18.7 %slice-start.3 = ((s8[16777216]{0:T(1024)(128)(4,1)}), s8[4194304]{0:T(1024)(128)(4,1)S(1)}, s32[]{:S(2)}) async-start(s8[16777216]{0:T(1024)(128)(4,1)} %bitcast.92), calls=%async_computation.9 | async-start | bytes 8388608
  129.0 169.8 %all-reduce.9.cloned.1.call-start = ((), (), s32[]{:S(2)}) async-start(), calls=%async_computation.1 | async-start | bytes 4194304 | tf_op jit(solution)/shard_map/psum | solution.py:57
  248.0 127.0 %all-reduce.11.cloned.1.call-start = ((), (), s32[]{:S(2)}) async-start(), calls=%async_computation.2 | async-start | bytes 524288 | tf_op jit(solution)/shard_map/psum | solution.py:58
  303.7 204.1 %all-reduce.13.cloned.1.call-start = ((), (), s32[]{:S(2)}) async-start(), calls=%async_computation.3 | async-start | bytes 4194304 | tf_op jit(solution)/shard_map/psum | solution.py:54
  382.5 2.0 copy-start
  406.1 101.7 %copy-start.1 = (f32[2048,256]{0,1:T(8,128)S(1)}, f32[2048,256]{0,1:T(8,128)}, u32[]{:S(2)}) copy-start(f32[2048,256]{0,1:T(8,128)} %all-reduce.7.cloned.1.call-done) | copy-start | bytes 6291460
  406.1 174.5 %all-reduce.15.cloned.1.call-start = ((), (), s32[]{:S(2)}) async-start(), calls=%async_computation.4 | async-start | bytes 4194304 | tf_op jit(solution)/shard_map/psum | solution.py:57
  510.7 1.3 copy-start.2
  529.8 127.0 %all-reduce.17.cloned.1.call-start = ((), (), s32[]{:S(2)}) async-start(), calls=%async_computation.5 | async-start | bytes 524288 | tf_op jit(solution)/shard_map/psum | solution.py:58
  664.4 2.0 copy-start.4
Sparse Core Ops, SparseCore 0:
  129.1 99.3 all-reduce.6
  248.1 50.6 all-reduce.8
  303.8 71.0 all-reduce.10
  406.2 101.5 all-reduce.12
  529.9 50.6 all-reduce.14
  585.7 71.0 all-reduce.16
